TPU v7x, 32 devices: a whole 2x2x4 slice. The times are simulated.
32 devices in a mesh: seq: 32 (over z, y, x, core).
Axes of the slice: x: 2, y: 2, z: 4, core: 2. Of those that a mesh axis runs over, the one named last changes fastest.
Arguments:
- tokens: bfloat16 [4, 2048, 768], P(None, 'seq'), may hold values from -6 to 6
- doc_lengths: int32 [4, 16], replicated, may hold values from 1 to 512, 2048 in all within a row
- first_gain: float32 [768], replicated, may hold values from 0.5 to 1.5
- first_shift: float32 [768], replicated, may hold values from -1.75 to 1.75
- input_weight: bfloat16 [768, 2304], replicated, may hold values from -0.21875 to 0.21875
- input_bias: float32 [2304], replicated, may hold values from -1.75 to 1.75
- short_kernel: float32 [3, 2304], replicated, may hold values from -3.5 to 3.5
- short_bias: float32 [2304], replicated, may hold values from -1.75 to 1.75
- embed_weight: float32 [33, 64], replicated, may hold values from -2 to 2
- embed_bias: float32 [64], replicated, may hold values from -3.140625 to 3.140625
- inner_weight: float32 [64, 64], replicated, may hold values from -1.5 to 1.5
- inner_bias: float32 [64], replicated, may hold values from -3.140625 to 3.140625
- filter_weight: float32 [64, 768], replicated, may hold values from -0.03125 to 0.03125
- decay_rates: float32 [768], replicated, may hold values from 3.07 to 15.35
- filter_bias: float32 [768], replicated, may hold values from -3 to 3
- output_weight: bfloat16 [768, 768], replicated, may hold values from -0.21875 to 0.21875
- output_bias: float32 [768], replicated, may hold values from -1.75 to 1.75
- second_gain: float32 [768], replicated, may hold values from 0.5 to 1.5
- second_shift: float32 [768], replicated, may hold values from -1.75 to 1.75
- up_weight: bfloat16 [768, 3072], replicated, may hold values from -0.21875 to 0.21875
- up_bias: float32 [3072], replicated, may hold values from -1.75 to 1.75
- down_weight: bfloat16 [3072, 768], replicated, may hold values from -0.109375 to 0.109375
- down_bias: float32 [768], replicated, may hold values from -1.75 to 1.75
- cotangent: bfloat16 [4, 2048, 768], P(None, 'seq'), may hold values from -6 to 6
Outputs:
- output: bfloat16 [4, 2048, 768], P(None, 'seq')
- grad_tokens: bfloat16 [4, 2048, 768], P(None, 'seq')
- grad_first_gain: float32 [768], replicated
- grad_first_shift: float32 [768], replicated
- grad_input_weight: float32 [768, 2304], replicated
- grad_input_bias: float32 [2304], replicated
- grad_short_kernel: float32 [3, 2304], replicated
- grad_short_bias: float32 [2304], replicated
- grad_embed_weight: float32 [33, 64], replicated
- grad_embed_bias: float32 [64], replicated
- grad_inner_weight: float32 [64, 64], replicated
- grad_inner_bias: float32 [64], replicated
- grad_filter_weight: float32 [64, 768], replicated
- grad_decay_rates: float32 [768], replicated
- grad_filter_bias: float32 [768], replicated
- grad_output_weight: float32 [768, 768], replicated
- grad_output_bias: float32 [768], replicated
- grad_second_gain: float32 [768], replicated
- grad_second_shift: float32 [768], replicated
- grad_up_weight: float32 [768, 3072], replicated
- grad_up_bias: float32 [3072], replicated
- grad_down_weight: float32 [3072, 768], replicated
- grad_down_bias: float32 [768], replicated
Inputs may be any that keep to these rules, and one draw needn't show every extreme that they name: `doc_lengths`: the lengths of one sequence add up to 2048, and the longest document of each sequence has exactly 512 positions.
All inputs are finite; a program needn't handle non-finite values.
Results may differ from a plain program's by a relative error of at most 0.014.
Values may be sent and summed in bfloat16 or wider, within the bound.
A program may use at most 192 MiB of HBM per device.

v0:
```python
import functools
import math
import jax
import jax.numpy as jnp
from jax import lax
from jax.sharding import PartitionSpec as P

HIGHEST_PRECISION = lax.Precision.HIGHEST
EPSILON = 1e-05


def from_behind(block, axis, distance):
    devices = range(lax.axis_size(axis))
    route = [(i - distance, i) for i in devices if i - distance in devices]
    return lax.ppermute(block, axis, route)


def shortened(x):
    return jax.tree.map(lambda a: a.astype(jnp.bfloat16) if a.dtype == jnp.float32 else a, x)


def layer_norm(values, norm_gain, norm_shift):
    center = values - jnp.mean(values, axis=-1, keepdims=True)
    spread = jnp.mean(center * center, axis=-1, keepdims=True)
    return center * lax.rsqrt(spread + EPSILON) * norm_gain + norm_shift


def embed_positions(positions, length, embed_width):
    band_count = (embed_width - 1) // 2
    harmonic = jnp.arange(1, band_count + 1, dtype=jnp.int32)
    phases = positions[:, None] * harmonic[None, :] % length
    angles = 2.0 * math.pi / length * phases.astype(jnp.float32)
    scaled = positions.astype(jnp.float32)[:, None] / length
    return jnp.concatenate([scaled, jnp.cos(angles), jnp.sin(angles)], axis=1)


def build_filter(
    embed_weight,
    embed_bias,
    inner_weight,
    inner_bias,
    filter_weight,
    decay_rates,
    embedded=None,
    scaled_positions=None,
):
    first_hidden = jnp.sin(
        jnp.dot(embedded, embed_weight, precision=HIGHEST_PRECISION) + embed_bias
    )
    second_hidden = jnp.sin(
        jnp.dot(first_hidden, inner_weight, precision=HIGHEST_PRECISION) + inner_bias
    )
    raw_filter = jnp.dot(second_hidden, filter_weight, precision=HIGHEST_PRECISION)
    return raw_filter * jnp.exp(-decay_rates[None, :] * scaled_positions[:, None])


def dft_tables(half_count, column_count):
    full_count = 2 * half_count
    total_count = full_count * column_count
    first_rows = jnp.arange(half_count, dtype=jnp.int32)
    first_freqs = jnp.arange(full_count, dtype=jnp.int32)
    second_index = jnp.arange(column_count, dtype=jnp.int32)
    first_angles = (
        2.0
        * math.pi
        / full_count
        * (first_rows[:, None] * first_freqs[None, :] % full_count).astype(jnp.float32)
    )
    second_angles = (
        2.0
        * math.pi
        / column_count
        * (second_index[:, None] * second_index[None, :] % column_count).astype(jnp.float32)
    )
    twist_angles = (
        2.0
        * math.pi
        / total_count
        * (first_freqs[:, None] * second_index[None, :] % total_count).astype(jnp.float32)
    )
    return (
        jnp.cos(first_angles),
        jnp.sin(first_angles),
        jnp.cos(second_angles),
        jnp.sin(second_angles),
        jnp.cos(twist_angles)[:, :, None],
        jnp.sin(twist_angles)[:, :, None],
    )


def first_section(values, matrix):
    return jnp.einsum("...nbc,nk->...kbc", values, matrix, precision=HIGHEST_PRECISION)


def first_back(values, matrix):
    return jnp.einsum("...kbc,nk->...nbc", values, matrix, precision=HIGHEST_PRECISION)


def second_section(values, matrix):
    return jnp.einsum("...kbc,bj->...kjc", values, matrix, precision=HIGHEST_PRECISION)


def second_back(values, matrix):
    return jnp.einsum("...kjc,bj->...kbc", values, matrix, precision=HIGHEST_PRECISION)


def forward_spectrum(values, tables):
    first_cos, first_sin, second_cos, second_sin, twist_cos, twist_sin = tables
    half_count = first_cos.shape[0]
    column_count = second_cos.shape[0]
    shaped = values.reshape(values.shape[:-2] + (half_count, column_count, values.shape[-1]))
    real_one = first_section(shaped, first_cos)
    imag_one = -first_section(shaped, first_sin)
    real_two = real_one * twist_cos + imag_one * twist_sin
    imag_two = imag_one * twist_cos - real_one * twist_sin
    real_out = second_section(real_two, second_cos) + second_section(imag_two, second_sin)
    imag_out = second_section(imag_two, second_cos) - second_section(real_two, second_sin)
    return (real_out, imag_out)


def inverse_half(real_in, imag_in, tables):
    first_cos, first_sin, second_cos, second_sin, twist_cos, twist_sin = tables
    half_count = first_cos.shape[0]
    column_count = second_cos.shape[0]
    real_one = second_back(real_in, second_cos) - second_back(imag_in, second_sin)
    imag_one = second_back(imag_in, second_cos) + second_back(real_in, second_sin)
    real_two = real_one * twist_cos - imag_one * twist_sin
    imag_two = imag_one * twist_cos + real_one * twist_sin
    result = first_back(real_two, first_cos) - first_back(imag_two, first_sin)
    result = result * (1.0 / (2 * half_count * column_count))
    return result.reshape(result.shape[:-3] + (half_count * column_count, result.shape[-1]))


def shards(
    tokens,
    doc_lengths,
    first_gain,
    first_shift,
    input_weight,
    input_bias,
    short_kernel,
    short_bias,
    embed_weight,
    embed_bias,
    inner_weight,
    inner_bias,
    filter_weight,
    decay_rates,
    filter_bias,
    output_weight,
    output_bias,
    second_gain,
    second_shift,
    up_weight,
    up_bias,
    down_weight,
    down_bias,
    cotangent,
):
    row_count, local_count, model_width = tokens.shape
    stream_width = 3 * model_width
    device_count = lax.axis_size("seq")
    seq_length = local_count * device_count
    offset = lax.axis_index("seq") * local_count
    positions = offset + jnp.arange(local_count, dtype=jnp.int32)
    doc_ends = jnp.cumsum(doc_lengths, axis=1)[:, :-1]
    starting = jnp.any(positions[None, :, None] == doc_ends[:, None, :], axis=-1) | (
        positions[None, :] == 0
    )
    keep_one = jnp.where(starting, 0.0, 1.0).astype(jnp.float32)
    keep_two = keep_one * jnp.concatenate(
        [jnp.ones((row_count, 1), jnp.float32), keep_one[:, :-1]], axis=1
    )
    keep_one_col = keep_one[:, :, None]
    keep_two_col = keep_two[:, :, None]
    token_values = tokens.astype(jnp.float32)
    first_norm, first_pullback = jax.vjp(layer_norm, token_values, first_gain, first_shift)
    normed = first_norm.astype(jnp.bfloat16)
    projected = (
        jnp.einsum("rsd,de->rse", normed, input_weight, preferred_element_type=jnp.float32)
        + input_bias
    ).astype(jnp.bfloat16)
    rim_rows = jnp.concatenate(
        [projected[:, -2:-1] * keep_one_col[:, -1:].astype(jnp.bfloat16), projected[:, -1:]], axis=1
    )
    previous = from_behind(rim_rows, "seq", 1)
    extended = jnp.concatenate([previous, projected], axis=1).astype(jnp.float32)
    lag_one = extended[:, 1:-1]
    lag_two = extended[:, :-2]
    proj_values = extended[:, 2:]
    short_out = (
        short_kernel[0] * proj_values
        + short_kernel[1] * keep_one_col * lag_one
        + short_kernel[2] * keep_two_col * lag_two
        + short_bias
    )
    gate_zero = short_out[..., :model_width]
    gate_one = short_out[..., model_width : 2 * model_width]
    value_part = short_out[..., 2 * model_width :]
    gated = value_part * gate_one
    tables = dft_tables(local_count, device_count)
    embedded = embed_positions(positions, seq_length, embed_weight.shape[0])
    scaled_positions = positions.astype(jnp.float32) / seq_length
    filter_fn = functools.partial(
        build_filter, embedded=embedded, scaled_positions=scaled_positions
    )
    filter_rows, filter_pullback = jax.vjp(
        filter_fn, embed_weight, embed_bias, inner_weight, inner_bias, filter_weight, decay_rates
    )
    spread_gated, spread_filter = (
        lax.all_to_all(
            gated.astype(jnp.bfloat16), "seq", split_axis=2, concat_axis=1, tiled=True
        ).astype(gated.dtype),
        lax.all_to_all(
            filter_rows[None].astype(jnp.bfloat16), "seq", split_axis=2, concat_axis=1, tiled=True
        ).astype(jnp.float32),
    )
    spread_filter = spread_filter[0]
    gated_real, gated_imag = forward_spectrum(spread_gated, tables)
    filter_real, filter_imag = forward_spectrum(spread_filter[None], tables)
    conv_real = gated_real * filter_real - gated_imag * filter_imag
    conv_imag = gated_real * filter_imag + gated_imag * filter_real
    conv_columns = inverse_half(conv_real, conv_imag, tables)
    conv_rows = lax.all_to_all(
        shortened(conv_columns), "seq", split_axis=1, concat_axis=2, tiled=True
    ).astype(conv_columns.dtype)
    conv_full = conv_rows + filter_bias * gated
    mixed_low = (conv_full * gate_zero).astype(jnp.bfloat16)
    branch = (
        jnp.einsum("rsd,de->rse", mixed_low, output_weight, preferred_element_type=jnp.float32)
        + output_bias
    )
    residual = token_values + branch
    second_norm, second_pullback = jax.vjp(layer_norm, residual, second_gain, second_shift)
    normed_two = second_norm.astype(jnp.bfloat16)
    pre_active = (
        jnp.einsum("rsd,df->rsf", normed_two, up_weight, preferred_element_type=jnp.float32)
        + up_bias
    )
    activated, gelu_pullback = jax.vjp(functools.partial(jax.nn.gelu, approximate=True), pre_active)
    hidden = activated.astype(jnp.bfloat16)
    output = (
        residual
        + jnp.einsum("rsf,fd->rsd", hidden, down_weight, preferred_element_type=jnp.float32)
        + down_bias
    ).astype(jnp.bfloat16)
    cot_values = cotangent.astype(jnp.float32)
    grad_down_weight = jnp.einsum(
        "rsf,rsd->fd", hidden, cotangent, preferred_element_type=jnp.float32
    )
    grad_down_bias = jnp.sum(cot_values, axis=(0, 1))
    grad_hidden = jnp.einsum(
        "rsd,fd->rsf", cotangent, down_weight, preferred_element_type=jnp.float32
    )
    grad_pre = gelu_pullback(grad_hidden)[0].astype(jnp.bfloat16)
    grad_up_weight = jnp.einsum(
        "rsd,rsf->df", normed_two, grad_pre, preferred_element_type=jnp.float32
    )
    grad_up_bias = jnp.sum(grad_pre.astype(jnp.float32), axis=(0, 1))
    grad_normed_two = jnp.einsum(
        "rsf,df->rsd", grad_pre, up_weight, preferred_element_type=jnp.float32
    )
    grad_residual_part, grad_second_gain, grad_second_shift = second_pullback(grad_normed_two)
    grad_residual = cot_values + grad_residual_part
    grad_branch = grad_residual.astype(jnp.bfloat16)
    grad_output_weight = jnp.einsum(
        "rsd,rse->de", mixed_low, grad_branch, preferred_element_type=jnp.float32
    )
    grad_output_bias = jnp.sum(grad_branch.astype(jnp.float32), axis=(0, 1))
    grad_mixed = jnp.einsum(
        "rse,de->rsd", grad_branch, output_weight, preferred_element_type=jnp.float32
    )
    grad_conv = grad_mixed * gate_zero
    grad_gate_zero = grad_mixed * conv_full
    grad_filter_bias = jnp.sum(grad_conv * gated, axis=(0, 1))
    grad_conv_columns = lax.all_to_all(
        grad_conv.astype(jnp.bfloat16), "seq", split_axis=2, concat_axis=1, tiled=True
    ).astype(grad_conv.dtype)
    grad_real, grad_imag = forward_spectrum(grad_conv_columns, tables)
    back_real = filter_real * grad_real + filter_imag * grad_imag
    back_imag = filter_real * grad_imag - filter_imag * grad_real
    grad_gated_columns = inverse_half(back_real, back_imag, tables)
    taps_real = jnp.sum(gated_real * grad_real + gated_imag * grad_imag, axis=0, keepdims=True)
    taps_imag = jnp.sum(gated_real * grad_imag - gated_imag * grad_real, axis=0, keepdims=True)
    grad_filter_columns = inverse_half(taps_real, taps_imag, tables)
    grad_gated_rows, grad_filter_rows = (
        lax.all_to_all(
            shortened(grad_gated_columns), "seq", split_axis=1, concat_axis=2, tiled=True
        ).astype(grad_gated_columns.dtype),
        lax.all_to_all(
            shortened(grad_filter_columns), "seq", split_axis=1, concat_axis=2, tiled=True
        ).astype(grad_filter_columns.dtype),
    )
    filter_grads = filter_pullback(grad_filter_rows[0])
    grad_filter_weight = filter_grads[4]
    grad_decay_rates = filter_grads[5]
    grad_gated = grad_gated_rows + filter_bias * grad_conv
    grad_short = jnp.concatenate(
        [grad_gate_zero, grad_gated * value_part, grad_gated * gate_one], axis=-1
    )
    grad_short_bias = jnp.sum(grad_short, axis=(0, 1))
    grad_short_kernel = jnp.stack(
        [
            jnp.sum(grad_short * proj_values, axis=(0, 1)),
            jnp.sum(grad_short * keep_one_col * lag_one, axis=(0, 1)),
            jnp.sum(grad_short * keep_two_col * lag_two, axis=(0, 1)),
        ]
    )
    tap_one = short_kernel[1] * keep_one_col * grad_short
    tap_two = short_kernel[2] * keep_two_col * grad_short
    outgoing = jnp.concatenate([tap_two[:, 0:1], tap_one[:, 0:1] + tap_two[:, 1:2]], axis=1)
    incoming = from_behind(shortened(outgoing), "seq", -1).astype(outgoing.dtype)
    grad_proj = (
        short_kernel[0] * grad_short
        + jnp.concatenate(
            [tap_one[:, 1:], jnp.zeros((row_count, 1, stream_width), jnp.float32)], axis=1
        )
        + jnp.concatenate(
            [tap_two[:, 2:], jnp.zeros((row_count, 2, stream_width), jnp.float32)], axis=1
        )
    )
    rim_terms = jnp.concatenate(
        [
            jnp.zeros((row_count, local_count - 2, stream_width), jnp.float32),
            incoming[:, 0:1] * keep_one_col[:, -1:],
            incoming[:, 1:2],
        ],
        axis=1,
    )
    grad_proj_low = (grad_proj + rim_terms).astype(jnp.bfloat16)
    grad_input_weight = jnp.einsum(
        "rsd,rse->de", normed, grad_proj_low, preferred_element_type=jnp.float32
    )
    grad_input_bias = jnp.sum(grad_proj_low.astype(jnp.float32), axis=(0, 1))
    grad_normed = jnp.einsum(
        "rse,de->rsd", grad_proj_low, input_weight, preferred_element_type=jnp.float32
    )
    grad_token_part, grad_first_gain, grad_first_shift = first_pullback(grad_normed)
    grad_tokens = (grad_residual + grad_token_part).astype(jnp.bfloat16)
    summed = lax.psum(
        (
            grad_first_gain,
            grad_first_shift,
            grad_input_weight,
            grad_input_bias,
            grad_short_kernel,
            grad_short_bias,
            filter_grads[0],
            filter_grads[1],
            filter_grads[2],
            filter_grads[3],
            grad_filter_weight,
            grad_decay_rates,
            grad_filter_bias,
            grad_output_weight,
            grad_output_bias,
            grad_second_gain,
            grad_second_shift,
            grad_up_weight,
            grad_up_bias,
            grad_down_weight,
            grad_down_bias,
        ),
        "seq",
    )
    summed = tuple(summed)
    return (output, grad_tokens) + summed


def solution(mesh):
    return jax.shard_map(
        shards,
        mesh=mesh,
        in_specs=(
            P(None, "seq", None),
            P(),
            P(),
            P(),
            P(),
            P(),
            P(),
            P(),
            P(),
            P(),
            P(),
            P(),
            P(),
            P(),
            P(),
            P(),
            P(),
            P(),
            P(),
            P(),
            P(),
            P(),
            P(),
            P(None, "seq", None),
        ),
        out_specs=(
            P(None, "seq", None),
            P(None, "seq", None),
            P(),
            P(),
            P(),
            P(),
            P(),
            P(),
            P(),
            P(),
            P(),
            P(),
            P(),
            P(),
            P(),
            P(),
            P(),
            P(),
            P(),
            P(),
            P(),
            P(),
            P(),
        ),
        check_vma=False,
    )
```

profile of v0, /device:TPU:0, one launch (start us, length us, event | category | flops | bytes accessed | tf_op | source)
XLA Modules:
  0.0 992.1 jit_solution(14004255950969521183)
XLA Ops:
  22.4 7.4 all-to-all-start.1
  50.0 8.3 all-to-all-start
  101.9 5.5 copy.287
  107.3 6.6 reshape.376
  113.9 5.7 all-to-all-start.2
  121.5 11.3 %all-to-all-done.2 = bf16[32,2,3072]{2,1,0:T(2,128)(2,1)} async-done(((bf16[32,2,3072]{2,1,0:T(2,128)(2,1)}), bf16[32,2,3072]{2,1,0:T(2,128)(2,1)}, u32[]{:S(2)}, u32[]{:S(2)}) %all-to-all-start.2) | async-done | bytes 393248 | tf_op jit(solution)/shard_map/all_to_all | solution.py:224
  132.8 7.7 reshape.377
  160.5 7.0 convert_reduce_fusion
  169.7 5.3 convolution_bitcast_fusion.1
  194.1 7.0 convolution_bitcast_fusion
  236.8 4.1 reshape.366
  240.9 13.4 %reduce.11 = bf16[2048,24]{1,0:T(8,128)(2,1)} reduce(bf16[2048,1,24]{2,1,0:T(2,128)(2,1)} %bitcast.425, bf16[]{:T(256)} %broadcast.460), dimensions={1}, to_apply=%bitcast.363.reduce_sub_computation | reduce | bytes 196610
  260.2 4.4 convolution_add_fusion.1
  270.4 5.5 copy.292
  275.8 6.6 reshape.380
  282.4 6.1 all-to-all-start.4
  288.6 4.0 reshape.383
  312.0 7.7 reshape.381
  347.4 5.6 convolution_bitcast_fusion.2
  353.8 6.1 fusion.93
  359.9 143.6 %all-reduce.8.cloned.1.call-done = (f32[768]{0:T(1024)}, f32[768]{0:T(1024)}, f32[2304]{0:T(1024)}, f32[3,2304]{1,0:T(4,128)}, f32[2304]{0:T(1024)}, /*index=5*/...) async-done(((f32[768]{0:T(1024)}, f32[768]{0:T(1024)}, ...) | async-done | bytes 108304 | tf_op jit(solution)/shard_map/psum | solution.py:340
  503.5 449.5 %all-reduce.10.cloned.1.call-done = (f32[768,2304]{1,0:T(8,128)}, f32[64,768]{1,0:T(8,128)}, f32[768,768]{1,0:T(8,128)}, f32[768,3072]{1,0:T(8,128)}, f32[3072,768]{1,0:T(8,128)}) async-done(((f32[768,2304]{1,0:T(8,128)}, f32[64,768]{1,0:T(8,128)}, f32[768,768]{1,0:T(8,128)}, f32[768,3072]{1,0:T(8,128)}, f32[3072,768]{1,0:T(8,128)}), (f32[768,2304]{1,0:T(8,128)}, f32[64,768]{1,0:T(8,128)}, ...) | async-done | bytes 28508176 | tf_op jit(solution)/shard_map/psum | solution.py:340
  955.6 6.6 copy.321
  971.4 8.8 copy.336
  (397 shorter events, 232.7 us)
Async XLA Ops:
  7.2 28.7 %copy-start = (bf16[768,2304]{1,0:T(8,128)(2,1)S(1)}, bf16[768,2304]{1,0:T(8,128)(2,1)}, u32[]{:S(2)}) copy-start(bf16[768,2304]{1,0:T(8,128)(2,1)} %param.28) | copy-start | bytes 10616836
  11.6 21.1 %copy-start.98 = (s32[4,16]{1,0:T(4,128)S(1)}, s32[4,16]{1,0:T(4,128)}, u32[]{:S(2)}) copy-start(s32[4,16]{1,0:T(4,128)} %param.25) | copy-start | bytes 772
  22.4 27.6 %all-to-all-start.1 = ((bf16[32,2,768]{2,1,0:T(2,128)(2,1)}), bf16[32,2,768]{2,1,0:T(2,128)(2,1)}, u32[]{:S(2)}, u32[]{:S(2)}) async-start(bf16[32,2,768]{2,1,0:T(2,128)(2,1)} %reshape.374), calls=%async_computation.1 | async-start | bytes 196608 | tf_op jit(solution)/shard_map/all_to_all | solution.py:214
  38.3 3.0 collective-permute-start
  50.0 21.5 %all-to-all-start = ((bf16[32,2,3072]{2,1,0:T(2,128)(2,1)}), bf16[32,2,3072]{2,1,0:T(2,128)(2,1)}, u32[]{:S(2)}, u32[]{:S(2)}) async-start(bf16[32,2,3072]{2,1,0:T(2,128)(2,1)} %reshape.372), calls=%async_computation | async-start | bytes 786432 | tf_op jit(solution)/shard_map/all_to_all | solution.py:211
  113.9 18.8 %all-to-all-start.2 = ((bf16[32,2,3072]{2,1,0:T(2,128)(2,1)}), bf16[32,2,3072]{2,1,0:T(2,128)(2,1)}, u32[]{:S(2)}, u32[]{:S(2)}) async-start(bf16[32,2,3072]{2,1,0:T(2,128)(2,1)} %reshape.376), calls=%async_computation.2 | async-start | bytes 786432 | tf_op jit(solution)/shard_map/all_to_all | solution.py:224
  156.2 18.8 %copy-start.20 = (f32[4,64,768]{2,1,0:T(8,128)}, f32[4,64,768]{2,1,0:T(8,128)S(1)}, u32[]{:S(2)}) copy-start(f32[4,64,768]{2,1,0:T(8,128)S(1)} %get-tuple-element.86) | copy-start | bytes 2359300
  156.5 11.0 %slice-start.3 = ((s8[4718592]{0:T(1024)(128)(4,1)}), s8[4194304]{0:T(1024)(128)(4,1)S(1)}, s32[]{:S(2)}) async-start(s8[4718592]{0:T(1024)(128)(4,1)} %bitcast.423), calls=%async_computation.11 | async-start | bytes 8388608
  187.2 16.9 %all-to-all-start.3 = ((bf16[32,2,3072]{2,1,0:T(2,128)(2,1)}), bf16[32,2,3072]{2,1,0:T(2,128)(2,1)}, u32[]{:S(2)}, u32[]{:S(2)}) async-start(bf16[32,2,3072]{2,1,0:T(2,128)(2,1)} %reshape.378), calls=%async_computation.3 | async-start | bytes 786432 | tf_op jit(solution)/shard_map/all_to_all | solution.py:276
  256.7 25.7 %all-to-all-start.5 = ((bf16[32,2,768]{2,1,0:T(2,128)(2,1)}), bf16[32,2,768]{2,1,0:T(2,128)(2,1)}, u32[]{:S(2)}, u32[]{:S(2)}) async-start(bf16[32,2,768]{2,1,0:T(2,128)(2,1)} %reshape.382), calls=%async_computation.5 | async-start | bytes 196608 | tf_op jit(solution)/shard_map/all_to_all | solution.py:290
  282.4 29.5 %all-to-all-start.4 = ((bf16[32,2,3072]{2,1,0:T(2,128)(2,1)}), bf16[32,2,3072]{2,1,0:T(2,128)(2,1)}, u32[]{:S(2)}, u32[]{:S(2)}) async-start(bf16[32,2,3072]{2,1,0:T(2,128)(2,1)} %reshape.380), calls=%async_computation.4 | async-start | bytes 786432 | tf_op jit(solution)/shard_map/all_to_all | solution.py:287
  288.5 215.0 %all-reduce.8.cloned.1.call-start = ((), (), s32[]{:S(2)}) async-start(), calls=%async_computation.6 | async-start | bytes 321536 | tf_op jit(solution)/shard_map/psum | solution.py:340
  295.9 10.9 %copy-start.58 = (f32[64,16]{0,1:T(8,128)S(1)}, f32[64,16]{0,1:T(8,128)}, u32[]{:S(2)}) copy-start(f32[64,16]{0,1:T(8,128)} %copy-done.57) | copy-start | bytes 12292
  337.9 3.1 collective-permute-start.1
  347.2 605.8 %all-reduce.10.cloned.1.call-start = ((), (), s32[]{:S(2)}) async-start(), calls=%async_computation.7 | async-start | bytes 57016320 | tf_op jit(solution)/shard_map/psum | solution.py:340
  955.6 9.6 copy-start.67
  955.6 10.2 %copy-start.102 = (f32[64]{0:T(128)S(1)}, f32[64]{0:T(128)}, u32[]{:S(2)}) copy-start(f32[64]{0:T(128)} %get-tuple-element.109) | copy-start | bytes 772
  955.6 10.7 %copy-start.47 = (f32[64,768]{1,0:T(8,128)S(1)}, f32[64,768]{1,0:T(8,128)}, u32[]{:S(2)}) copy-start(f32[64,768]{1,0:T(8,128)} %get-tuple-element.110) | copy-start | bytes 589828
  955.6 11.4 %copy-start.94 = (f32[768]{0:T(1024)S(1)}, f32[768]{0:T(1024)}, u32[]{:S(2)}) copy-start(f32[768]{0:T(1024)} %get-tuple-element.111) | copy-start | bytes 9220
  955.6 12.0 %copy-start.93 = (f32[768]{0:T(1024)S(1)}, f32[768]{0:T(1024)}, u32[]{:S(2)}) copy-start(f32[768]{0:T(1024)} %get-tuple-element.112) | copy-start | bytes 9220
  955.6 12.5 %copy-start.37 = (f32[768,768]{1,0:T(8,128)S(1)}, f32[768,768]{1,0:T(8,128)}, u32[]{:S(2)}) copy-start(f32[768,768]{1,0:T(8,128)} %get-tuple-element.113) | copy-start | bytes 7077892
  968.2 12.6 %slice-start = ((s8[9437184]{0:T(1024)(128)(4,1)}), s8[4194304]{0:T(1024)(128)(4,1)S(1)}, s32[]{:S(2)}) async-start(s8[9437184]{0:T(1024)(128)(4,1)} %bitcast.413), calls=%async_computation.8 | async-start | bytes 8388608
  971.4 9.4 slice-start.1
  971.4 9.4 slice-start.2
  (95 other events, 292.8 us)
Sparse Core Ops, SparseCore 0:
  347.3 156.1 all-reduce.7
  513.1 439.8 all-reduce.9
where the time goes:
time: 1000 us; the launch traced here: 992 us
  waiting for transfers between devices  609 us (61%)
  local copies, waits for them, and re-layouts  166 us (17%)
  matrix products  121 us (12%)
  other arithmetic  42.1 us (4%)
  starting transfers between devices  38.3 us (4%)
  between operations  15.8 us (2%)
    psum x2, waiting for transfers between devices, shards(): lax.psum((grad_first_gain, grad_first_shift, grad_input_weight, grad_inpu...  593 us
    unnamed x253, local copies, waits for them, and re-layouts  90.6 us
    dot_general x12, matrix products, second_back(): jnp.einsum('...kjc,bj->...kbc', values, matrix, precision=HIGHEST_PRECISION)  20.8 us
  transfers between devices with their start and end apart: 10, of which 6 were waited for; matrix products, arithmetic and copies ran while one was open for 10% of the time, Pallas kernels for 0%

commit v1 on v0

--- a/solution.py
+++ b/solution.py
@@ -7,6 +7,15 @@
 
 HIGHEST_PRECISION = lax.Precision.HIGHEST
 EPSILON = 1e-05
+
+
+def raise_the_knots(local_x):
+    return jnp.concatenate(
+        jax.lax.all_to_all(
+            jnp.stack(jnp.split(local_x, jax.lax.axis_size("seq"), axis=1)), "seq", 0, 0
+        ),
+        axis=2,
+    )
 
 
 def from_behind(block, axis, distance):
@@ -221,9 +230,7 @@
     conv_real = gated_real * filter_real - gated_imag * filter_imag
     conv_imag = gated_real * filter_imag + gated_imag * filter_real
     conv_columns = inverse_half(conv_real, conv_imag, tables)
-    conv_rows = lax.all_to_all(
-        shortened(conv_columns), "seq", split_axis=1, concat_axis=2, tiled=True
-    ).astype(conv_columns.dtype)
+    conv_rows = raise_the_knots(shortened(conv_columns)).astype(conv_columns.dtype)
     conv_full = conv_rows + filter_bias * gated
     mixed_low = (conv_full * gate_zero).astype(jnp.bfloat16)
     branch = (

time: 1000 us -> 1030 us (1.030)
  local copies, waits for them, and re-layouts: 166 us -> 194 us
    unnamed x253 -> x284, local copies, waits for them, and re-layouts: 90.6 us -> 125 us
where the time goes in v1:
time: 1030 us; the launch traced here: 1020 us
  waiting for transfers between devices  609 us (59%)
  local copies, waits for them, and re-layouts  194 us (19%)
  matrix products  121 us (12%)
  other arithmetic  43.5 us (4%)
  starting transfers between devices  38.4 us (4%)
  between operations  15.8 us (2%)
    psum x2, waiting for transfers between devices, shards(): lax.psum((grad_first_gain, grad_first_shift, grad_input_weight, grad_inpu...  593 us
    unnamed x284, local copies, waits for them, and re-layouts  125 us
    dot_general x12, matrix products, second_back(): jnp.einsum('...kjc,bj->...kbc', values, matrix, precision=HIGHEST_PRECISION)  20.7 us
  transfers between devices with their start and end apart: 10, of which 6 were waited for; matrix products, arithmetic and copies ran while one was open for 10% of the time, Pallas kernels for 0%

profile of v1, /device:TPU:0, one launch (start us, length us, event | category | flops | bytes accessed | tf_op | source)
XLA Modules:
  0.0 1020.9 jit_solution(8745569360675244281)
XLA Ops:
  22.4 7.4 all-to-all-start.1
  50.0 8.7 all-to-all-start
  155.2 5.8 all-to-all-start.2
  163.0 11.3 %all-to-all-done.2 = bf16[32,2,3072]{2,1,0:T(2,128)(2,1)} async-done(((bf16[32,2,3072]{2,1,0:T(2,128)(2,1)}), bf16[32,2,3072]{2,1,0:T(2,128)(2,1)}, u32[]{:S(2)}, u32[]{:S(2)}) %all-to-all-start.2) | async-done | bytes 393248 | tf_op jit(solution)/shard_map/all_to_all | solution.py:14
  185.3 4.0 fusion.8
  189.3 7.0 convert_reduce_fusion
  198.5 5.3 convolution_bitcast_fusion.1
  222.5 7.0 convolution_bitcast_fusion
  265.6 4.1 reshape.365
  269.7 13.4 %reduce.11 = bf16[2048,24]{1,0:T(8,128)(2,1)} reduce(bf16[2048,1,24]{2,1,0:T(2,128)(2,1)} %bitcast.553, bf16[]{:T(256)} %broadcast.460), dimensions={1}, to_apply=%bitcast.493.reduce_sub_computation | reduce | bytes 196610
  289.0 4.4 convolution_add_fusion.1
  299.1 5.5 copy.316
  304.6 6.6 reshape.379
  311.2 6.1 all-to-all-start.4
  317.3 4.0 reshape.382
  340.7 7.7 reshape.380
  348.5 3.9 copy.273
  376.2 5.6 convolution_bitcast_fusion.2
  382.5 6.1 fusion.93
  388.7 143.6 %all-reduce.8.cloned.1.call-done = (f32[768]{0:T(1024)}, f32[768]{0:T(1024)}, f32[2304]{0:T(1024)}, f32[3,2304]{1,0:T(4,128)}, f32[2304]{0:T(1024)}, /*index=5*/...) async-done(((f32[768]{0:T(1024)}, f32[768]{0:T(1024)}, ...) | async-done | bytes 108304 | tf_op jit(solution)/shard_map/psum | solution.py:347
  532.3 449.5 %all-reduce.10.cloned.1.call-done = (f32[768,2304]{1,0:T(8,128)}, f32[64,768]{1,0:T(8,128)}, f32[768,768]{1,0:T(8,128)}, f32[768,3072]{1,0:T(8,128)}, f32[3072,768]{1,0:T(8,128)}) async-done(((f32[768,2304]{1,0:T(8,128)}, f32[64,768]{1,0:T(8,128)}, f32[768,768]{1,0:T(8,128)}, f32[768,3072]{1,0:T(8,128)}, f32[3072,768]{1,0:T(8,128)}), (f32[768,2304]{1,0:T(8,128)}, f32[64,768]{1,0:T(8,128)}, ...) | async-done | bytes 28508176 | tf_op jit(solution)/shard_map/psum | solution.py:347
  984.4 6.6 copy.375
  1000.2 8.8 copy.390
  1009.5 3.7 copy.392
  (429 shorter events, 269.1 us)
Async XLA Ops:
  7.2 28.7 %copy-start = (bf16[768,2304]{1,0:T(8,128)(2,1)S(1)}, bf16[768,2304]{1,0:T(8,128)(2,1)}, u32[]{:S(2)}) copy-start(bf16[768,2304]{1,0:T(8,128)(2,1)} %param.28) | copy-start | bytes 10616836
  11.6 21.1 %copy-start.98 = (s32[4,16]{1,0:T(4,128)S(1)}, s32[4,16]{1,0:T(4,128)}, u32[]{:S(2)}) copy-start(s32[4,16]{1,0:T(4,128)} %param.25) | copy-start | bytes 772
  22.4 27.6 %all-to-all-start.1 = ((bf16[32,2,768]{2,1,0:T(2,128)(2,1)}), bf16[32,2,768]{2,1,0:T(2,128)(2,1)}, u32[]{:S(2)}, u32[]{:S(2)}) async-start(bf16[32,2,768]{2,1,0:T(2,128)(2,1)} %reshape.373), calls=%async_computation.1 | async-start | bytes 196608 | tf_op jit(solution)/shard_map/all_to_all | solution.py:223
  38.3 3.0 collective-permute-start
  50.0 21.8 %all-to-all-start = ((bf16[32,2,3072]{2,1,0:T(2,128)(2,1)}), bf16[32,2,3072]{2,1,0:T(2,128)(2,1)}, u32[]{:S(2)}, u32[]{:S(2)}) async-start(bf16[32,2,3072]{2,1,0:T(2,128)(2,1)} %reshape.371), calls=%async_computation | async-start | bytes 786432 | tf_op jit(solution)/shard_map/all_to_all | solution.py:220
  155.2 19.0 %all-to-all-start.2 = ((bf16[32,2,3072]{2,1,0:T(2,128)(2,1)}), bf16[32,2,3072]{2,1,0:T(2,128)(2,1)}, u32[]{:S(2)}, u32[]{:S(2)}) async-start(bf16[32,2,3072]{2,1,0:T(2,128)(2,1)} %reshape.375), calls=%async_computation.2 | async-start | bytes 786432 | tf_op jit(solution)/shard_map/all_to_all | solution.py:14
  185.0 18.8 %copy-start.20 = (f32[4,64,768]{2,1,0:T(8,128)}, f32[4,64,768]{2,1,0:T(8,128)S(1)}, u32[]{:S(2)}) copy-start(f32[4,64,768]{2,1,0:T(8,128)S(1)} %get-tuple-element.86) | copy-start | bytes 2359300
  185.3 11.0 %slice-start.3 = ((s8[4718592]{0:T(1024)(128)(4,1)}), s8[4194304]{0:T(1024)(128)(4,1)S(1)}, s32[]{:S(2)}) async-start(s8[4718592]{0:T(1024)(128)(4,1)} %bitcast.551), calls=%async_computation.11 | async-start | bytes 8388608
  216.0 16.5 %all-to-all-start.3 = ((bf16[32,2,3072]{2,1,0:T(2,128)(2,1)}), bf16[32,2,3072]{2,1,0:T(2,128)(2,1)}, u32[]{:S(2)}, u32[]{:S(2)}) async-start(bf16[32,2,3072]{2,1,0:T(2,128)(2,1)} %reshape.377), calls=%async_computation.3 | async-start | bytes 786432 | tf_op jit(solution)/shard_map/all_to_all | solution.py:283
  285.5 25.7 %all-to-all-start.5 = ((bf16[32,2,768]{2,1,0:T(2,128)(2,1)}), bf16[32,2,768]{2,1,0:T(2,128)(2,1)}, u32[]{:S(2)}, u32[]{:S(2)}) async-start(bf16[32,2,768]{2,1,0:T(2,128)(2,1)} %reshape.381), calls=%async_computation.5 | async-start | bytes 196608 | tf_op jit(solution)/shard_map/all_to_all | solution.py:297
  311.2 29.5 %all-to-all-start.4 = ((bf16[32,2,3072]{2,1,0:T(2,128)(2,1)}), bf16[32,2,3072]{2,1,0:T(2,128)(2,1)}, u32[]{:S(2)}, u32[]{:S(2)}) async-start(bf16[32,2,3072]{2,1,0:T(2,128)(2,1)} %reshape.379), calls=%async_computation.4 | async-start | bytes 786432 | tf_op jit(solution)/shard_map/all_to_all | solution.py:294
  317.3 215.0 %all-reduce.8.cloned.1.call-start = ((), (), s32[]{:S(2)}) async-start(), calls=%async_computation.6 | async-start | bytes 321536 | tf_op jit(solution)/shard_map/psum | solution.py:347
  324.7 10.9 %copy-start.58 = (f32[64,16]{0,1:T(8,128)S(1)}, f32[64,16]{0,1:T(8,128)}, u32[]{:S(2)}) copy-start(f32[64,16]{0,1:T(8,128)} %copy-done.57) | copy-start | bytes 12292
  366.7 3.1 collective-permute-start.1
  376.0 605.8 %all-reduce.10.cloned.1.call-start = ((), (), s32[]{:S(2)}) async-start(), calls=%async_computation.7 | async-start | bytes 57016320 | tf_op jit(solution)/shard_map/psum | solution.py:347
  984.3 9.6 copy-start.67
  984.4 10.2 copy-start.102
  984.4 10.7 %copy-start.47 = (f32[64,768]{1,0:T(8,128)S(1)}, f32[64,768]{1,0:T(8,128)}, u32[]{:S(2)}) copy-start(f32[64,768]{1,0:T(8,128)} %get-tuple-element.110) | copy-start | bytes 589828
  984.4 11.4 %copy-start.94 = (f32[768]{0:T(1024)S(1)}, f32[768]{0:T(1024)}, u32[]{:S(2)}) copy-start(f32[768]{0:T(1024)} %get-tuple-element.111) | copy-start | bytes 9220
  984.4 12.0 %copy-start.93 = (f32[768]{0:T(1024)S(1)}, f32[768]{0:T(1024)}, u32[]{:S(2)}) copy-start(f32[768]{0:T(1024)} %get-tuple-element.112) | copy-start | bytes 9220
  984.4 12.5 %copy-start.37 = (f32[768,768]{1,0:T(8,128)S(1)}, f32[768,768]{1,0:T(8,128)}, u32[]{:S(2)}) copy-start(f32[768,768]{1,0:T(8,128)} %get-tuple-element.113) | copy-start | bytes 7077892
  996.9 12.6 %slice-start = ((s8[9437184]{0:T(1024)(128)(4,1)}), s8[4194304]{0:T(1024)(128)(4,1)S(1)}, s32[]{:S(2)}) async-start(s8[9437184]{0:T(1024)(128)(4,1)} %bitcast.544), calls=%async_computation.8 | async-start | bytes 8388608
  1000.2 9.4 slice-start.1
  1000.2 9.4 slice-start.2
  (95 other events, 292.7 us)
Sparse Core Ops, SparseCore 0:
  376.1 156.1 all-reduce.7
  541.9 439.8 all-reduce.9
